TPU v7x, 256 devices: a whole 4x4x8 slice. The times are simulated.
256 devices in a mesh: ep: 16 (over x, y), dp: 16 (over z, core).
Axes of the slice: x: 4, y: 4, z: 8, core: 2. Of those that a mesh axis runs over, the one named last changes fastest.
Arguments:
- tokens: float32 [32768, 1024], P(('ep', 'dp')), may hold values from -6 to 6
- cotangent: float32 [32768, 1024], P(('ep', 'dp')), may hold values from -6 to 6
- w_gate: float32 [256, 1024, 256], P(('ep', 'dp')), may hold values from -0.1875 to 0.1875
- w_up: float32 [256, 1024, 256], P(('ep', 'dp')), may hold values from -0.1875 to 0.1875
- w_down: float32 [256, 256, 1024], P(('ep', 'dp')), may hold values from -0.25 to 0.25
- expert_ids: int32 [32768, 2], P(('ep', 'dp')), may hold values from 0 to 127, as said below
- route_weight: float32 [32768, 2], P(('ep', 'dp')), may hold values from 0.25 to 1
- halted: int32 [32768], P(('ep', 'dp')), may hold values 0 or 1
Outputs:
- grad_x: float32 [32768, 1024], P(('ep', 'dp'))
- grad_gate: float32 [256, 1024, 256], P(('ep', 'dp'))
- grad_up: float32 [256, 1024, 256], P(('ep', 'dp'))
- grad_down: float32 [256, 256, 1024], P(('ep', 'dp'))
Inputs may be any that keep to these rules, and one draw needn't show every extreme that they name: `expert_ids`: within the rows of one device the two ids of a token differ, no expert is named more than 3 times, and every expert whose number is a multiple of 8 is named exactly 3 times.
All inputs are finite; a program needn't handle non-finite values. No bound on the sum of `halted` on one device may be relied on, other than what follows from the above.
Results may differ from a plain program's by a relative error of at most 0.0003.
Values sent between devices are 32-bit elements; how exact they have to be, the bound alone decides.
A program may use at most 128 MiB of HBM per device.

v0:
```python
import jax
import jax.numpy as jnp
from jax import lax
from jax.sharding import PartitionSpec as P

block_rows = 128
highest = lax.Precision.HIGHEST


def expert_grads(x_rows, d_rows, w_gate, w_upper, w_down):
    gate_value = jnp.dot(x_rows, w_gate, precision=highest)
    upper_value = jnp.dot(x_rows, w_upper, precision=highest)
    sigmoid_gate = jax.nn.sigmoid(gate_value)
    active = gate_value * sigmoid_gate
    hidden = active * upper_value
    d_hidden = jnp.dot(d_rows, w_down.T, precision=highest)
    d_gate = d_hidden * upper_value * sigmoid_gate * (1.0 + gate_value * (1.0 - sigmoid_gate))
    d_upper = d_hidden * active
    g_gate = jnp.dot(x_rows.T, d_gate, precision=highest)
    g_upper = jnp.dot(x_rows.T, d_upper, precision=highest)
    g_down = jnp.dot(hidden.T, d_rows, precision=highest)
    d_input = jnp.dot(d_gate, w_gate.T, precision=highest) + jnp.dot(
        d_upper, w_upper.T, precision=highest
    )
    return (g_gate, g_upper, g_down, d_input)


def fill_slots(source, tokens, cotangent, route_rows, flag_rows):
    token_of = source // 2
    x_slots = jnp.take(tokens, token_of, axis=0, mode="fill", fill_value=0.0)
    d_slots = jnp.take(cotangent, token_of, axis=0, mode="fill", fill_value=0.0)
    weights = jnp.take(route_rows, source, axis=0, mode="fill", fill_value=0.0)
    flags = jnp.take(flag_rows, source, axis=0, mode="fill", fill_value=0.0)
    return (x_slots, d_slots * weights[:, None], flags)


def expert_backward(x_rows, d_rows, live_flags, w_gate, w_upper, w_down):
    row_count, model_width = x_rows.shape
    padded = -(-row_count // block_rows) * block_rows
    live_int = (live_flags > 0.5).astype(jnp.int32)
    packed_at = jnp.cumsum(live_int) - live_int
    live_total = jnp.sum(live_int)
    target = jnp.where(live_int > 0, packed_at, padded)
    source = (
        jnp.full((padded + 1,), row_count, jnp.int32)
        .at[target]
        .set(jnp.arange(row_count, dtype=jnp.int32))[:padded]
    )
    packed_x = jnp.take(x_rows, source, axis=0, mode="fill", fill_value=0.0)
    packed_d = jnp.take(d_rows, source, axis=0, mode="fill", fill_value=0.0)
    block_total = (live_total + block_rows - 1) // block_rows
    start_state = (
        jnp.zeros(w_gate.shape, jnp.float32),
        jnp.zeros(w_upper.shape, jnp.float32),
        jnp.zeros(w_down.shape, jnp.float32),
        jnp.zeros((padded, model_width), jnp.float32),
    )

    def block_step(block_index, state):
        block_start = block_index * block_rows
        x_block = lax.dynamic_slice_in_dim(packed_x, block_start, block_rows, 0)
        d_block = lax.dynamic_slice_in_dim(packed_d, block_start, block_rows, 0)
        g_gate, g_upper, g_down, d_input = expert_grads(x_block, d_block, w_gate, w_upper, w_down)
        return (
            state[0] + g_gate,
            state[1] + g_upper,
            state[2] + g_down,
            lax.dynamic_update_slice_in_dim(state[3], d_input, block_start, 0),
        )

    finished = lax.fori_loop(0, block_total, block_step, start_state)
    back_rows = jnp.take(finished[3], jnp.minimum(target, padded - 1), axis=0) * live_int[
        :, None
    ].astype(jnp.float32)
    return (finished[0], finished[1], finished[2], back_rows)


def local(tokens, cotangent, w_gate, w_up, w_down, expert_ids, route_weight, halted):
    ep_count = lax.axis_size("ep")
    dp_count = lax.axis_size("dp")
    token_count, model_width = tokens.shape
    row_total = 2 * token_count
    group_experts = dp_count // 2
    expert_count = ep_count * group_experts
    slot_most = 3 * token_count // expert_count
    flat_ids = expert_ids.reshape(-1)
    owner_index = flat_ids // group_experts
    local_index = flat_ids % group_experts
    one_hot = (flat_ids[:, None] == jnp.arange(expert_count, dtype=jnp.int32)[None, :]).astype(
        jnp.int32
    )
    slot_rank = jnp.sum((jnp.cumsum(one_hot, axis=0) - one_hot) * one_hot, axis=1)
    live_tokens = (1 - halted).astype(jnp.float32)
    route_rows = (route_weight * live_tokens[:, None]).reshape(-1)
    flag_rows = jnp.ones_like(route_rows)
    own_gate = w_gate[0]
    own_upper = w_up[0]
    own_down = w_down[0]
    slot_total = ep_count * dp_count * slot_most
    dest_low = (owner_index * dp_count + 2 * local_index) * slot_most + slot_rank
    dest = jnp.concatenate([dest_low, dest_low + slot_most])
    table = jnp.full((slot_total + 1,), row_total, jnp.int32)
    row_numbers = jnp.arange(row_total, dtype=jnp.int32)
    source = table.at[dest].set(jnp.concatenate([row_numbers, row_numbers]))[:slot_total]
    x_slots, d_slots, f_slots = fill_slots(source, tokens, cotangent, route_rows, flag_rows)
    send_x = x_slots.reshape(ep_count, dp_count, slot_most * model_width)
    send_d = d_slots.reshape(ep_count, dp_count, slot_most * model_width)
    send_f = f_slots.reshape(ep_count, dp_count, slot_most)
    held_x, held_d, held_f = (
        lax.all_to_all(
            lax.all_to_all(send_x, "ep", split_axis=0, concat_axis=0, tiled=True),
            "dp",
            split_axis=1,
            concat_axis=1,
            tiled=True,
        ),
        lax.all_to_all(
            lax.all_to_all(send_d, "ep", split_axis=0, concat_axis=0, tiled=True),
            "dp",
            split_axis=1,
            concat_axis=1,
            tiled=True,
        ),
        lax.all_to_all(
            lax.all_to_all(send_f, "ep", split_axis=0, concat_axis=0, tiled=True),
            "dp",
            split_axis=1,
            concat_axis=1,
            tiled=True,
        ),
    )
    g_gate, g_upper, g_down, back_rows = expert_backward(
        held_x.reshape(-1, model_width),
        held_d.reshape(-1, model_width),
        held_f.reshape(-1),
        own_gate,
        own_upper,
        own_down,
    )
    returned = lax.all_to_all(
        lax.all_to_all(
            back_rows.reshape(ep_count, dp_count, slot_most * model_width),
            "ep",
            split_axis=0,
            concat_axis=0,
            tiled=True,
        ),
        "dp",
        split_axis=1,
        concat_axis=1,
        tiled=True,
    )
    joined = returned.reshape(ep_count, group_experts, 2, slot_most * model_width).sum(axis=2)
    contrib = joined.reshape(ep_count, group_experts, slot_most, model_width)[
        owner_index, local_index, slot_rank
    ]
    grad_x = cotangent + contrib.reshape(token_count, 2, model_width).sum(axis=1)
    return (grad_x, g_gate[None], g_upper[None], g_down[None])


def solution(mesh):
    in_specs = (
        P(("ep", "dp"), None),
        P(("ep", "dp"), None),
        P(("ep", "dp"), None, None),
        P(("ep", "dp"), None, None),
        P(("ep", "dp"), None, None),
        P(("ep", "dp"), None),
        P(("ep", "dp"), None),
        P(("ep", "dp")),
    )
    out_specs = (
        P(("ep", "dp"), None),
        P(("ep", "dp"), None, None),
        P(("ep", "dp"), None, None),
        P(("ep", "dp"), None, None),
    )
    return jax.shard_map(local, mesh=mesh, in_specs=in_specs, out_specs=out_specs, check_vma=False)
```

profile of v0, /device:TPU:1, one launch (start us, length us, event | category | flops | bytes accessed | tf_op | source)
XLA Modules:
  0.0 611.0 jit_solution(17021105274068658303)
XLA Ops:
  2.4 2.4 scatter_custom_fusion
  6.5 5.0 gather_fusion.6
  11.5 5.0 gather_fusion.2
  17.5 7.6 %all-to-all-start = ((f32[16,16,3]{1,2,0:T(4,128)}), f32[16,16,3]{1,2,0:T(4,128)S(1)}, u32[]{:S(2)}, u32[]{:S(2)}) async-start(f32[16,16,3]{1,2,0:T(4,128)} %copy.66), calls=%async_computation | async-start | bytes 65536 | tf_op jit(solution)/shard_map/all_to_all | solution.py:125
  25.1 3.7 gather_fusion.5
  28.8 3.6 gather_fusion.3
  33.1 9.7 %all-to-all-start.1 = ((f32[16,16,3]{0,2,1:T(4,128)}), f32[16,16,3]{0,2,1:T(4,128)S(1)}, u32[]{:S(2)}, u32[]{:S(2)}) async-start(f32[16,16,3]{0,2,1:T(4,128)} %copy.67), calls=%async_computation.1 | async-start | bytes 65536 | tf_op jit(solution)/shard_map/all_to_all | solution.py:124
  42.9 5.9 select_multiply_fusion
  48.8 4.9 reshape.407
  53.7 6.7 %all-to-all-start.2 = ((f32[16,16,3072]{2,1,0:T(8,128)}), f32[16,16,3072]{2,1,0:T(8,128)}, u32[]{:S(2)}, u32[]{:S(2)}) async-start(f32[16,16,3072]{2,1,0:T(8,128)} %reshape.407), calls=%async_computation.2 | async-start | bytes 6291456 | tf_op jit(solution)/shard_map/all_to_all | solution.py:111
  60.4 5.0 reshape.410
  65.4 36.1 %all-to-all-done.2 = f32[16,16,3072]{2,1,0:T(8,128)} async-done(((f32[16,16,3072]{2,1,0:T(8,128)}), f32[16,16,3072]{2,1,0:T(8,128)}, u32[]{:S(2)}, u32[]{:S(2)}) %all-to-all-start.2) | async-done | bytes 3145760 | tf_op jit(solution)/shard_map/all_to_all | solution.py:111
  101.5 11.9 %all-to-all-start.4 = ((f32[16,16,3072]{2,1,0:T(8,128)}), f32[16,16,3072]{2,1,0:T(8,128)}, u32[]{:S(2)}, u32[]{:S(2)}) async-start(f32[16,16,3072]{2,1,0:T(8,128)} %reshape.410), calls=%async_computation.4 | async-start | bytes 6291456 | tf_op jit(solution)/shard_map/all_to_all | solution.py:118
  113.4 5.3 copy.73
  118.7 34.9 %all-to-all-done.4 = f32[16,16,3072]{2,1,0:T(8,128)} async-done(((f32[16,16,3072]{2,1,0:T(8,128)}), f32[16,16,3072]{2,1,0:T(8,128)}, u32[]{:S(2)}, u32[]{:S(2)}) %all-to-all-start.4) | async-done | bytes 3145760 | tf_op jit(solution)/shard_map/all_to_all | solution.py:118
  153.7 8.6 %all-to-all-start.3 = ((f32[16,16,3072]{2,0,1:T(8,128)}), f32[16,16,3072]{2,0,1:T(8,128)}, u32[]{:S(2)}, u32[]{:S(2)}) async-start(f32[16,16,3072]{2,0,1:T(8,128)} %copy.73), calls=%async_computation.3 | async-start | bytes 6291456 | tf_op jit(solution)/shard_map/all_to_all | solution.py:110
  162.3 5.4 copy.76
  167.7 65.7 %all-to-all-done.3 = f32[16,16,3072]{2,0,1:T(8,128)} async-done(((f32[16,16,3072]{2,0,1:T(8,128)}), f32[16,16,3072]{2,0,1:T(8,128)}, u32[]{:S(2)}, u32[]{:S(2)}) %all-to-all-start.3) | async-done | bytes 3145760 | tf_op jit(solution)/shard_map/all_to_all | solution.py:110
  233.3 6.1 all-to-all-start.5
  242.5 2.5 mul.147
  245.1 6.1 %mul.148 = f32[16,16,3072]{2,1,0:T(8,128)} reshape(f32[16,16,3,1024]{3,2,1,0:T(4,128)} %mul.147) | data formatting | bytes 6291456 | tf_op jit(solution)/shard_map/mul | solution.py:72
  252.1 3.1 broadcast_in_dim.79
  255.4 3.4 scatter_custom_fusion.1
  258.8 5.3 copy.74
  264.2 4.7 reshape.408
  268.8 41.5 %all-to-all-done.5 = f32[16,16,3072]{2,0,1:T(8,128)} async-done(((f32[16,16,3072]{2,0,1:T(8,128)}), f32[16,16,3072]{2,0,1:T(8,128)}, u32[]{:S(2)}, u32[]{:S(2)}) %all-to-all-start.5) | async-done | bytes 3145760 | tf_op jit(solution)/shard_map/all_to_all | solution.py:117
  310.3 5.4 copy.77
  315.7 4.6 reshape.411
  320.3 6.5 %gather_fusion.4 = f32[768,1024]{1,0:T(8,128)} fusion(f32[768,1024]{1,0:T(8,128)} %reshape.408, s32[1024]{0:T(1024)S(1)} %pad_clamp_fusion.1), kind=kCustom, calls=%fused_computation.2.clone | custom fusion | bytes 6294528 | tf_op jit(solution)/shard_map/jit(_take)/gather | solution.py:49
  326.8 6.6 %gather_fusion.7 = f32[768,1024]{1,0:T(8,128)} fusion(f32[768,1024]{1,0:T(8,128)} %reshape.411, s32[1024]{0:T(1024)S(1)} %pad_clamp_fusion.1), kind=kCustom, calls=%fused_computation.5.clone | custom fusion | bytes 6294528 | tf_op jit(solution)/shard_map/jit(_take)/gather | solution.py:50
  333.4 5.9 broadcast_select_fusion
  344.6 113.0 %while.16 = (s32[]{:T(128)}, f32[1024,256]{1,0:T(8,128)}, f32[1024,256]{1,0:T(8,128)}, f32[256,1024]{1,0:T(8,128)}, f32[768,1024]{1,0:T(8,128)}, /*index=5*/s32[...) while((s32[]{:T(128)}, f32[1024,256]{1,0:T(8,128)}, ...), condition=%wide.region_9.13_spmd, body=%wide.region_8.12_spmd.sunk | while | flops 3223224320 | bytes 39190884 | solution.py:71
  348.3 2.3 fusion.89
  353.8 2.5 convolution_add_fusion.7
  356.3 2.8 convolution_add_fusion.8
  360.2 3.4 convolution_add_fusion.9
  367.1 2.3 fusion.89
  372.6 2.5 convolution_add_fusion.7
  375.1 2.8 convolution_add_fusion.8
  379.0 3.4 convolution_add_fusion.9
  385.9 2.3 fusion.89
  391.4 2.5 convolution_add_fusion.7
  394.0 2.9 convolution_add_fusion.8
  397.8 3.4 convolution_add_fusion.9
  404.7 2.3 fusion.89
  410.2 2.5 convolution_add_fusion.7
  412.8 2.8 convolution_add_fusion.8
  416.6 3.4 convolution_add_fusion.9
  429.0 2.5 convolution_add_fusion.7
  431.6 2.8 convolution_add_fusion.8
  435.4 3.4 convolution_add_fusion.9
  442.3 2.3 fusion.89
  447.8 2.5 convolution_add_fusion.7
  450.4 2.9 convolution_add_fusion.8
  454.2 3.4 convolution_add_fusion.9
  457.6 6.6 %gather_fusion = f32[768,1024]{1,0:T(8,128)} fusion(f32[768,1024]{1,0:T(8,128)} %get-tuple-element.68, s32[1024]{0:T(1024)S(1)} %pad_clamp_fusion), kind=kCustom, calls=%fused_computation.6 | custom fusion | bytes 6294528 | tf_op jit(solution)/shard_map/jit(_take)/gather | solution.py:72
  464.2 5.0 gather.19
  469.2 3.4 select_multiply_fusion.1
  472.7 41.6 %all_to_all.40 = f32[16,16,3072]{2,1,0:T(8,128)S(1)} all-to-all(f32[16,16,3072]{2,1,0:T(8,128)S(1)} %select_multiply_fusion.1), channel_id=1, replica_groups=mesh['ep'=16,'dp'=16] {'ep'}, dimensions={0} | all-to-all | bytes 6291456 | tf_op jit(solution)/shard_map/all_to_all | solution.py:141
  514.2 3.5 copy.79
  517.7 7.4 %all-to-all-start.7 = ((f32[16,16,3072]{2,0,1:T(8,128)}), f32[16,16,3072]{2,0,1:T(8,128)}, u32[]{:S(2)}, u32[]{:S(2)}) async-start(f32[16,16,3072]{2,0,1:T(8,128)} %copy.79), calls=%async_computation.7 | async-start | bytes 6291456 | tf_op jit(solution)/shard_map/all_to_all | solution.py:140
  525.3 70.9 %all-to-all-done.7 = f32[16,16,3072]{2,0,1:T(8,128)} async-done(((f32[16,16,3072]{2,0,1:T(8,128)}), f32[16,16,3072]{2,0,1:T(8,128)}, u32[]{:S(2)}, u32[]{:S(2)}) %all-to-all-start.7) | async-done | bytes 3145760 | tf_op jit(solution)/shard_map/all_to_all | solution.py:140
  600.6 2.8 copy.82
  603.5 3.4 gather_fusion.1
  (164 shorter events, 70.4 us)
Async XLA Ops:
  0.6 28.2 %copy-start = (f32[128,1024]{1,0:T(8,128)S(1)}, f32[128,1024]{1,0:T(8,128)}, u32[]{:S(2)}) copy-start(f32[128,1024]{1,0:T(8,128)} %param.16) | copy-start | bytes 1572868
  11.5 13.6 %copy-start.2 = (f32[128,1024]{1,0:T(8,128)S(1)}, f32[128,1024]{1,0:T(8,128)}, u32[]{:S(2)}) copy-start(f32[128,1024]{1,0:T(8,128)} %param.17) | copy-start | bytes 1572868
  17.5 14.9 %all-to-all-start = ((f32[16,16,3]{1,2,0:T(4,128)}), f32[16,16,3]{1,2,0:T(4,128)S(1)}, u32[]{:S(2)}, u32[]{:S(2)}) async-start(f32[16,16,3]{1,2,0:T(4,128)} %copy.66), calls=%async_computation | async-start | bytes 65536 | tf_op jit(solution)/shard_map/all_to_all | solution.py:125
  33.1 20.5 %all-to-all-start.1 = ((f32[16,16,3]{0,2,1:T(4,128)}), f32[16,16,3]{0,2,1:T(4,128)S(1)}, u32[]{:S(2)}, u32[]{:S(2)}) async-start(f32[16,16,3]{0,2,1:T(4,128)} %copy.67), calls=%async_computation.1 | async-start | bytes 65536 | tf_op jit(solution)/shard_map/all_to_all | solution.py:124
  53.7 47.8 %all-to-all-start.2 = ((f32[16,16,3072]{2,1,0:T(8,128)}), f32[16,16,3072]{2,1,0:T(8,128)}, u32[]{:S(2)}, u32[]{:S(2)}) async-start(f32[16,16,3072]{2,1,0:T(8,128)} %reshape.407), calls=%async_computation.2 | async-start | bytes 6291456 | tf_op jit(solution)/shard_map/all_to_all | solution.py:111
  101.5 52.2 %all-to-all-start.4 = ((f32[16,16,3072]{2,1,0:T(8,128)}), f32[16,16,3072]{2,1,0:T(8,128)}, u32[]{:S(2)}, u32[]{:S(2)}) async-start(f32[16,16,3072]{2,1,0:T(8,128)} %reshape.410), calls=%async_computation.4 | async-start | bytes 6291456 | tf_op jit(solution)/shard_map/all_to_all | solution.py:118
  153.7 79.7 %all-to-all-start.3 = ((f32[16,16,3072]{2,0,1:T(8,128)}), f32[16,16,3072]{2,0,1:T(8,128)}, u32[]{:S(2)}, u32[]{:S(2)}) async-start(f32[16,16,3072]{2,0,1:T(8,128)} %copy.73), calls=%async_computation.3 | async-start | bytes 6291456 | tf_op jit(solution)/shard_map/all_to_all | solution.py:110
  233.3 77.0 %all-to-all-start.5 = ((f32[16,16,3072]{2,0,1:T(8,128)}), f32[16,16,3072]{2,0,1:T(8,128)}, u32[]{:S(2)}, u32[]{:S(2)}) async-start(f32[16,16,3072]{2,0,1:T(8,128)} %copy.76), calls=%async_computation.5 | async-start | bytes 6291456 | tf_op jit(solution)/shard_map/all_to_all | solution.py:117
  339.4 5.3 copy-start.3
  339.4 5.3 copy-start.4
  344.8 3.5 copy-start.9
  348.3 5.5 copy-start.5
  351.8 4.5 copy-start.7
  356.3 2.9 copy-start.6
  359.2 1.0 copy-start.8
  363.6 3.5 copy-start.9
  367.1 5.5 copy-start.5
  370.6 4.6 copy-start.7
  375.1 2.9 copy-start.6
  378.0 1.0 copy-start.8
  382.4 3.5 copy-start.9
  385.8 5.6 copy-start.5
  389.4 4.6 copy-start.7
  393.9 2.9 copy-start.6
  396.8 1.0 copy-start.8
  401.2 3.5 copy-start.9
  404.7 5.6 copy-start.5
  408.2 4.6 copy-start.7
  412.8 2.9 copy-start.6
  415.6 1.0 copy-start.8
  420.0 3.5 copy-start.9
  423.5 5.5 copy-start.5
  427.0 4.6 copy-start.7
  431.6 2.9 copy-start.6
  434.5 1.0 copy-start.8
  438.8 3.5 copy-start.9
  442.3 5.5 copy-start.5
  445.8 4.6 copy-start.7
  450.4 2.9 copy-start.6
  453.3 1.0 copy-start.8
  464.2 5.0 copy-start.10
  517.7 78.4 %all-to-all-start.7 = ((f32[16,16,3072]{2,0,1:T(8,128)}), f32[16,16,3072]{2,0,1:T(8,128)}, u32[]{:S(2)}, u32[]{:S(2)}) async-start(f32[16,16,3072]{2,0,1:T(8,128)} %copy.79), calls=%async_computation.7 | async-start | bytes 6291456 | tf_op jit(solution)/shard_map/all_to_all | solution.py:140
  603.5 7.3 %copy-start.1 = (f32[128,1024]{1,0:T(8,128)S(1)}, f32[128,1024]{1,0:T(8,128)}, u32[]{:S(2)}) copy-start(f32[128,1024]{1,0:T(8,128)} %param.16) | copy-start | bytes 1572868
where the time goes:
time: 622 us; the launch traced here: 611 us
  waiting for transfers between devices  249 us (40%)
  local copies, waits for them, and re-layouts  131 us (21%)
  matrix products  106 us (17%)
  starting transfers between devices  57.9 us (9%)
  blocking collectives  41.6 us (7%)
  other arithmetic  22.7 us (4%)
    all_to_all x1, waiting for transfers between devices, local(): lax.all_to_all(lax.all_to_all(back_rows.reshape(ep_count, dp_count, slot_...  70.9 us
    all_to_all x1, waiting for transfers between devices, local(): lax.all_to_all(lax.all_to_all(send_x, 'ep', split_axis=0, concat_axis=0,...  65.7 us
    all_to_all x1, blocking collectives, local(): lax.all_to_all(back_rows.reshape(ep_count, dp_count, slot_most * model_wi...  41.6 us
    all_to_all x1, waiting for transfers between devices, local(): lax.all_to_all(lax.all_to_all(send_d, 'ep', split_axis=0, concat_axis=0,...  41.5 us
    all_to_all x1, waiting for transfers between devices, local(): lax.all_to_all(send_x, 'ep', split_axis=0, concat_axis=0, tiled=True)  36.1 us
    all_to_all x1, waiting for transfers between devices, local(): lax.all_to_all(send_d, 'ep', split_axis=0, concat_axis=0, tiled=True)  34.9 us
    dot_general x6, matrix products, expert_grads(): g_down = jnp.dot(hidden.T, d_rows, precision=highest)  20.4 us
    dot_general x6, matrix products, expert_grads(): g_upper = jnp.dot(x_rows.T, d_upper, precision=highest)  17.1 us
  transfers between devices with their start and end apart: 7, of which 5 were waited for; matrix products, arithmetic and copies ran while one was open for 10% of the time, Pallas kernels for 0%

commit v1 on v0

--- a/solution.py
+++ b/solution.py
@@ -107,12 +107,20 @@
     send_d = d_slots.reshape(ep_count, dp_count, slot_most * model_width)
     send_f = f_slots.reshape(ep_count, dp_count, slot_most)
     held_x, held_d, held_f = (
-        lax.all_to_all(
-            lax.all_to_all(send_x, "ep", split_axis=0, concat_axis=0, tiled=True),
-            "dp",
-            split_axis=1,
-            concat_axis=1,
-            tiled=True,
+        jnp.concatenate(
+            lax.all_to_all(
+                jnp.stack(
+                    jnp.split(
+                        lax.all_to_all(send_x, "ep", split_axis=0, concat_axis=0, tiled=True),
+                        lax.axis_size("dp"),
+                        axis=1,
+                    )
+                ),
+                "dp",
+                0,
+                0,
+            ),
+            axis=1,
         ),
         lax.all_to_all(
             lax.all_to_all(send_d, "ep", split_axis=0, concat_axis=0, tiled=True),

time: 622 us -> 635 us (1.021)
  local copies, waits for them, and re-layouts: 131 us -> 161 us
  waiting for transfers between devices: 249 us -> 228 us
  blocking collectives: 41.6 us -> 55.5 us
  starting transfers between devices: 57.9 us -> 48.2 us
    unnamed x14 -> x29, local copies, waits for them, and re-layouts: 0.88 us -> 34.6 us
    all_to_all x1, waiting for transfers between devices: 34.9 us -> 4.26 us  [local(): lax.all_to_all(send_d, 'ep', split_axis=0, concat_axis=0, tiled=True)]
    all_to_all x0 -> x1, blocking collectives: none -> 13.9 us  [local(): lax.all_to_all(send_f, 'ep', split_axis=0, concat_axis=0, tiled=True)]
    all_to_all x2 -> x0, local copies, waits for them, and re-layouts: 10.7 us -> none  [the longest x1 5.34 us: local(): lax.all_to_all(send_x, 'ep', split_axis=0, concat_axis=0, tiled=True)]
    all_to_all x2 -> x1, starting transfers between devices: 16.2 us -> 8.79 us  [local(): lax.all_to_all(jnp.stack(jnp.split(lax.all_to_all(send_x, 'ep', split_axi...]
    all_to_all x1, waiting for transfers between devices: 0.01 us -> 7.38 us  [local(): lax.all_to_all(lax.all_to_all(send_f, 'ep', split_axis=0, concat_axis=0,...]
    another operation x9 -> x11, local copies, waits for them, and re-layouts: 2.64 us -> 9.52 us  [the longest x1 4.62 us: local(): held_x.reshape(-1, model_width)]
    all_to_all x2 -> x1, waiting for transfers between devices: 65.7 us -> 65.6 us  [local(): lax.all_to_all(jnp.stack(jnp.split(lax.all_to_all(send_x, 'ep', split_axi...]
  transfers between devices with their start and end apart: 7 -> 6, of which waited for: 5 -> 6; matrix products, arithmetic and copies ran while one was open for 10% -> 12% of each run, Pallas kernels for 0% -> 0%
where the time goes in v1:
time: 635 us; the launch traced here: 624 us
  waiting for transfers between devices  228 us (36%)
  local copies, waits for them, and re-layouts  161 us (25%)
  matrix products  106 us (17%)
  blocking collectives  55.5 us (9%)
  starting transfers between devices  48.2 us (8%)
  other arithmetic  22.7 us (4%)
    all_to_all x1, waiting for transfers between devices, local(): lax.all_to_all(lax.all_to_all(back_rows.reshape(ep_count, dp_count, slot_...  70.9 us
    all_to_all x1, waiting for transfers between devices, local(): lax.all_to_all(jnp.stack(jnp.split(lax.all_to_all(send_x, 'ep', split_axi...  65.6 us
    all_to_all x1, waiting for transfers between devices, local(): lax.all_to_all(lax.all_to_all(send_d, 'ep', split_axis=0, concat_axis=0,...  43.5 us
    all_to_all x1, blocking collectives, local(): lax.all_to_all(back_rows.reshape(ep_count, dp_count, slot_most * model_wi...  41.7 us
    all_to_all x1, waiting for transfers between devices, local(): lax.all_to_all(send_x, 'ep', split_axis=0, concat_axis=0, tiled=True)  36.1 us
    unnamed x29, local copies, waits for them, and re-layouts  34.6 us
    dot_general x6, matrix products, expert_grads(): g_down = jnp.dot(hidden.T, d_rows, precision=highest)  20.4 us
    dot_general x6, matrix products, expert_grads(): g_upper = jnp.dot(x_rows.T, d_upper, precision=highest)  17.1 us
  transfers between devices with their start and end apart: 6, of which 6 were waited for; matrix products, arithmetic and copies ran while one was open for 12% of the time, Pallas kernels for 0%

profile of v1, /device:TPU:1, one launch (start us, length us, event | category | flops | bytes accessed | tf_op | source)
XLA Modules:
  0.0 624.0 jit_solution(3739807316812184269)
XLA Ops:
  2.4 2.4 scatter_custom_fusion
  6.5 5.0 gather_fusion.6
  11.5 5.0 gather_fusion.2
  16.9 13.9 %all_to_all.40 = f32[16,16,3]{1,2,0:T(4,128)S(1)} all-to-all(f32[16,16,3]{1,2,0:T(4,128)S(1)} %copy.65), channel_id=1, replica_groups=mesh['ep'=16,'dp'=16] {'ep'}, dimensions={0} | all-to-all | bytes 6144 | tf_op jit(solution)/shard_map/all_to_all | solution.py:133
  31.5 10.6 %all-to-all-start.1 = ((f32[16,16,3]{0,2,1:T(4,128)}), f32[16,16,3]{0,2,1:T(4,128)S(1)}, u32[]{:S(2)}, u32[]{:S(2)}) async-start(f32[16,16,3]{0,2,1:T(4,128)} %copy.66), calls=%async_computation.1 | async-start | bytes 65536 | tf_op jit(solution)/shard_map/all_to_all | solution.py:132
  42.0 7.4 %all-to-all-done.1 = f32[16,16,3]{0,2,1:T(4,128)S(1)} async-done(((f32[16,16,3]{0,2,1:T(4,128)}), f32[16,16,3]{0,2,1:T(4,128)S(1)}, u32[]{:S(2)}, u32[]{:S(2)}) %all-to-all-start.1) | async-done | bytes 3104 | tf_op jit(solution)/shard_map/all_to_all | solution.py:132
  51.4 3.7 gather_fusion.5
  55.0 3.6 gather_fusion.3
  58.7 5.9 select_multiply_fusion
  64.6 5.0 reshape.407
  69.6 4.5 all-to-all-start.2
  74.1 5.0 reshape.410
  79.0 36.1 %all-to-all-done.2 = f32[16,16,3072]{2,1,0:T(8,128)} async-done(((f32[16,16,3072]{2,1,0:T(8,128)}), f32[16,16,3072]{2,1,0:T(8,128)}, u32[]{:S(2)}, u32[]{:S(2)}) %all-to-all-start.2) | async-done | bytes 3145760 | tf_op jit(solution)/shard_map/all_to_all | solution.py:114
  115.2 11.6 %all-to-all-start.4 = ((f32[16,16,3072]{2,1,0:T(8,128)}), f32[16,16,3072]{2,1,0:T(8,128)}, u32[]{:S(2)}, u32[]{:S(2)}) async-start(f32[16,16,3072]{2,1,0:T(8,128)} %reshape.410), calls=%async_computation.4 | async-start | bytes 6291456 | tf_op jit(solution)/shard_map/all_to_all | solution.py:126
  162.8 4.3 all-to-all-done.4
  167.0 8.8 %all-to-all-start.3 = ((f32[16,16,1,3072]{3,2,1,0:T(1,128)}), f32[16,16,1,3072]{3,2,1,0:T(1,128)}, u32[]{:S(2)}, u32[]{:S(2)}) async-start(f32[16,16,1,3072]{3,2,1,0:T(1,128)} %fusion.24), calls=%async_computation.3 | async-start | bytes 6291456 | tf_op jit(solution)/shard_map/all_to_all | solution.py:111
  175.8 5.3 copy.74
  181.2 65.6 %all-to-all-done.3 = f32[16,16,1,3072]{3,2,1,0:T(1,128)} async-done(((f32[16,16,1,3072]{3,2,1,0:T(1,128)}), f32[16,16,1,3072]{3,2,1,0:T(1,128)}, u32[]{:S(2)}, u32[]{:S(2)}) %all-to-all-start.3) | async-done | bytes 3145760 | tf_op jit(solution)/shard_map/all_to_all | solution.py:111
  246.8 5.4 all-to-all-start.5
  253.5 2.6 mul.147
  256.1 6.1 mul.148
  263.2 3.1 broadcast_in_dim.79
  266.3 3.4 scatter_custom_fusion.1
  269.7 5.4 copy.72
  275.1 4.6 reshape_reshape.3
  279.7 43.5 %all-to-all-done.5 = f32[16,16,3072]{2,0,1:T(8,128)} async-done(((f32[16,16,3072]{2,0,1:T(8,128)}), f32[16,16,3072]{2,0,1:T(8,128)}, u32[]{:S(2)}, u32[]{:S(2)}) %all-to-all-start.5) | async-done | bytes 3145760 | tf_op jit(solution)/shard_map/all_to_all | solution.py:125
  323.3 5.4 copy.75
  328.6 4.6 reshape.411
  333.2 6.5 %gather_fusion.4 = f32[768,1024]{1,0:T(8,128)} fusion(f32[768,1024]{1,0:T(8,128)} %reshape_reshape.3, s32[1024]{0:T(1024)S(1)} %pad_clamp_fusion.1), kind=kCustom, calls=%fused_computation.2.clone | custom fusion | bytes 6294528 | tf_op jit(solution)/shard_map/jit(_take)/gather | solution.py:49
  339.8 6.6 %gather_fusion.7 = f32[768,1024]{1,0:T(8,128)} fusion(f32[768,1024]{1,0:T(8,128)} %reshape.411, s32[1024]{0:T(1024)S(1)} %pad_clamp_fusion.1), kind=kCustom, calls=%fused_computation.5.clone | custom fusion | bytes 6294528 | tf_op jit(solution)/shard_map/jit(_take)/gather | solution.py:50
  346.4 5.9 broadcast_select_fusion
  357.6 113.0 %while.16 = (s32[]{:T(128)}, f32[1024,256]{1,0:T(8,128)}, f32[1024,256]{1,0:T(8,128)}, f32[256,1024]{1,0:T(8,128)}, f32[768,1024]{1,0:T(8,128)}, /*index=5*/s32[...) while((s32[]{:T(128)}, f32[1024,256]{1,0:T(8,128)}, ...), condition=%wide.region_9.13_spmd, body=%wide.region_8.12_spmd.sunk | while | flops 3223224320 | bytes 39190884 | solution.py:71
  361.3 2.3 fusion.105
  366.8 2.5 convolution_add_fusion.7
  369.3 2.8 convolution_add_fusion.8
  373.1 3.4 convolution_add_fusion.9
  380.0 2.3 fusion.105
  385.5 2.5 convolution_add_fusion.7
  388.1 2.8 convolution_add_fusion.8
  391.9 3.4 convolution_add_fusion.9
  398.8 2.3 fusion.105
  404.4 2.5 convolution_add_fusion.7
  406.9 2.9 convolution_add_fusion.8
  410.8 3.4 convolution_add_fusion.9
  417.7 2.3 fusion.105
  423.2 2.5 convolution_add_fusion.7
  425.7 2.8 convolution_add_fusion.8
  429.6 3.4 convolution_add_fusion.9
  442.0 2.5 convolution_add_fusion.7
  444.6 2.8 convolution_add_fusion.8
  448.4 3.4 convolution_add_fusion.9
  455.3 2.3 fusion.105
  460.8 2.5 convolution_add_fusion.7
  463.4 2.9 convolution_add_fusion.8
  467.2 3.4 convolution_add_fusion.9
  470.6 6.6 %gather_fusion = f32[768,1024]{1,0:T(8,128)} fusion(f32[768,1024]{1,0:T(8,128)} %get-tuple-element.68, s32[1024]{0:T(1024)S(1)} %get-tuple-element.110), kind=kCustom, calls=%fused_computation.6 | custom fusion | bytes 6294528 | tf_op jit(solution)/shard_map/jit(_take)/gather | solution.py:72
  477.2 5.0 gather.19
  482.2 3.4 select_multiply_fusion.1
  485.6 41.7 %all_to_all.41 = f32[16,16,3072]{2,1,0:T(8,128)S(1)} all-to-all(f32[16,16,3072]{2,1,0:T(8,128)S(1)} %select_multiply_fusion.1), channel_id=1, replica_groups=mesh['ep'=16,'dp'=16] {'ep'}, dimensions={0} | all-to-all | bytes 6291456 | tf_op jit(solution)/shard_map/all_to_all | solution.py:149
  527.3 3.5 copy.77
  530.8 7.3 %all-to-all-start.7 = ((f32[16,16,3072]{2,0,1:T(8,128)}), f32[16,16,3072]{2,0,1:T(8,128)}, u32[]{:S(2)}, u32[]{:S(2)}) async-start(f32[16,16,3072]{2,0,1:T(8,128)} %copy.77), calls=%async_computation.7 | async-start | bytes 6291456 | tf_op jit(solution)/shard_map/all_to_all | solution.py:148
  538.3 70.9 %all-to-all-done.7 = f32[16,16,3072]{2,0,1:T(8,128)} async-done(((f32[16,16,3072]{2,0,1:T(8,128)}), f32[16,16,3072]{2,0,1:T(8,128)}, u32[]{:S(2)}, u32[]{:S(2)}) %all-to-all-start.7) | async-done | bytes 3145760 | tf_op jit(solution)/shard_map/all_to_all | solution.py:148
  613.6 2.8 copy.80
  616.5 3.4 gather_fusion.1
  (177 shorter events, 105.8 us)
Async XLA Ops:
  0.6 54.4 %copy-start = (f32[128,1024]{1,0:T(8,128)S(1)}, f32[128,1024]{1,0:T(8,128)}, u32[]{:S(2)}) copy-start(f32[128,1024]{1,0:T(8,128)} %param.16) | copy-start | bytes 1572868
  11.5 39.9 %copy-start.2 = (f32[128,1024]{1,0:T(8,128)S(1)}, f32[128,1024]{1,0:T(8,128)}, u32[]{:S(2)}) copy-start(f32[128,1024]{1,0:T(8,128)} %param.17) | copy-start | bytes 1572868
  31.5 18.0 %all-to-all-start.1 = ((f32[16,16,3]{0,2,1:T(4,128)}), f32[16,16,3]{0,2,1:T(4,128)S(1)}, u32[]{:S(2)}, u32[]{:S(2)}) async-start(f32[16,16,3]{0,2,1:T(4,128)} %copy.66), calls=%async_computation.1 | async-start | bytes 65536 | tf_op jit(solution)/shard_map/all_to_all | solution.py:132
  69.6 45.6 %all-to-all-start.2 = ((f32[16,16,3072]{2,1,0:T(8,128)}), f32[16,16,3072]{2,1,0:T(8,128)}, u32[]{:S(2)}, u32[]{:S(2)}) async-start(f32[16,16,3072]{2,1,0:T(8,128)} %reshape.407), calls=%async_computation.2 | async-start | bytes 6291456 | tf_op jit(solution)/shard_map/all_to_all | solution.py:114
  115.2 51.9 %all-to-all-start.4 = ((f32[16,16,3072]{2,1,0:T(8,128)}), f32[16,16,3072]{2,1,0:T(8,128)}, u32[]{:S(2)}, u32[]{:S(2)}) async-start(f32[16,16,3072]{2,1,0:T(8,128)} %reshape.410), calls=%async_computation.4 | async-start | bytes 6291456 | tf_op jit(solution)/shard_map/all_to_all | solution.py:126
  167.0 79.7 %all-to-all-start.3 = ((f32[16,16,1,3072]{3,2,1,0:T(1,128)}), f32[16,16,1,3072]{3,2,1,0:T(1,128)}, u32[]{:S(2)}, u32[]{:S(2)}) async-start(f32[16,16,1,3072]{3,2,1,0:T(1,128)} %fusion.24), calls=%async_computation.3 | async-start | bytes 6291456 | tf_op jit(solution)/shard_map/all_to_all | solution.py:111
  246.8 76.5 %all-to-all-start.5 = ((f32[16,16,3072]{2,0,1:T(8,128)}), f32[16,16,3072]{2,0,1:T(8,128)}, u32[]{:S(2)}, u32[]{:S(2)}) async-start(f32[16,16,3072]{2,0,1:T(8,128)} %copy.74), calls=%async_computation.5 | async-start | bytes 6291456 | tf_op jit(solution)/shard_map/all_to_all | solution.py:125
  352.3 5.3 copy-start.3
  352.3 5.3 copy-start.4
  357.8 3.5 copy-start.9
  361.2 5.5 copy-start.5
  364.8 4.5 copy-start.7
  369.3 2.9 copy-start.6
  372.2 1.0 copy-start.8
  376.5 3.5 copy-start.9
  380.0 5.5 copy-start.5
  383.5 4.6 copy-start.7
  388.1 2.9 copy-start.6
  391.0 1.0 copy-start.8
  395.3 3.5 copy-start.9
  398.8 5.6 copy-start.5
  402.3 4.6 copy-start.7
  406.9 2.9 copy-start.6
  409.8 1.0 copy-start.8
  414.2 3.5 copy-start.9
  417.6 5.6 copy-start.5
  421.2 4.6 copy-start.7
  425.7 2.9 copy-start.6
  428.6 1.0 copy-start.8
  433.0 3.5 copy-start.9
  436.5 5.5 copy-start.5
  440.0 4.6 copy-start.7
  444.5 2.9 copy-start.6
  447.4 1.0 copy-start.8
  451.8 3.5 copy-start.9
  455.3 5.5 copy-start.5
  458.8 4.6 copy-start.7
  463.3 2.9 copy-start.6
  466.2 1.0 copy-start.8
  477.2 5.0 copy-start.10
  530.8 78.3 %all-to-all-start.7 = ((f32[16,16,3072]{2,0,1:T(8,128)}), f32[16,16,3072]{2,0,1:T(8,128)}, u32[]{:S(2)}, u32[]{:S(2)}) async-start(f32[16,16,3072]{2,0,1:T(8,128)} %copy.77), calls=%async_computation.7 | async-start | bytes 6291456 | tf_op jit(solution)/shard_map/all_to_all | solution.py:148
  616.4 7.3 %copy-start.1 = (f32[128,1024]{1,0:T(8,128)S(1)}, f32[128,1024]{1,0:T(8,128)}, u32[]{:S(2)}) copy-start(f32[128,1024]{1,0:T(8,128)} %param.16) | copy-start | bytes 1572868
